TPU v7x, 32 devices: a whole 2x2x4 slice. The times are simulated.
32 devices in a mesh: groups: 2 (over x), rows: 16 (over z, y, core).
Axes of the slice: x: 2, y: 2, z: 4, core: 2. Of those that a mesh axis runs over, the one named last changes fastest.
Arguments:
- block_input: bfloat16 [512, 352, 512], P(('groups', 'rows')), parts along dimension 0, may hold values from -6 to 6
- first_pre: bfloat16 [512, 352, 128], P(('groups', 'rows')), parts along dimension 0, may hold values from -6 to 6
- second_pre: bfloat16 [512, 352, 128], P(('groups', 'rows')), parts along dimension 0, may hold values from -6 to 6
- output_pre: bfloat16 [512, 352, 512], P(('groups', 'rows')), parts along dimension 0, may hold values from -6 to 6
- output_grad: bfloat16 [512, 352, 512], P('groups', None, 'rows'), parts along dimension 0, may hold values from -6 to 6
- first_weight: bfloat16 [512, 128], replicated, may hold values from -0.25 to 0.25
- middle_weight: bfloat16 [3, 3, 128, 128], replicated, may hold values from -0.1875 to 0.1875
- last_weight: bfloat16 [128, 512], replicated, may hold values from -0.5 to 0.5
Outputs:
- input_grad: bfloat16 [512, 352, 512], P(('groups', 'rows')), parts along dimension 0
- first_weight_grad: float32 [1024, 128], P(('groups', 'rows')), parts along dimension 0
- middle_weight_grad: float32 [6, 3, 128, 128], P('groups'), parts along dimension 0
- last_weight_grad: float32 [256, 512], P('groups'), parts along dimension 0
There are 2 independent parts, one for each index of `groups`. A program takes and returns all parts, laid end to end along the dimension named above; an argument that names none is the same for every part. Nothing has to cross between parts.
All inputs are finite; a program needn't handle non-finite values.
Results may differ from a plain program's by a relative error of at most 0.0049.
Values may be sent and summed in bfloat16 or wider, within the bound.
No kernel may reach another device: no remote copies, remote signals or barrier semaphores. Data moves between devices by JAX's collectives and lax.ppermute only.
A program may use at most 128 MiB of HBM per device.

v0:
```python
import math
import jax
import jax.numpy as jnp
from jax import lax
from jax.sharding import PartitionSpec as P


def with_halo(value, sides, width):
    for axis, dim in sides:
        size, length = (lax.axis_size(axis), value.shape[dim])
        up = [(i, (i + 1) % size) for i in range(size - 1)]
        down = [(j, i) for i, j in up]
        last = lax.slice_in_dim(value, length - width, length, axis=dim)
        leading = lax.slice_in_dim(value, 0, width, axis=dim)
        before = lax.ppermute(last, axis, up)
        after = lax.ppermute(leading, axis, down)
        value = jnp.concatenate([before, value, after], axis=dim)
    return value


def contract_rows(left, right):
    return lax.dot_general(
        left, right, (((0,), (0,)), ((), ())), preferred_element_type=jnp.float32
    )


def shards(
    block_input,
    first_pre,
    second_pre,
    output_pre,
    output_grad,
    first_weight,
    middle_weight,
    last_weight,
):
    tile_rows, map_cols, channels = block_input.shape
    inner_width = first_pre.shape[2]
    pixels = tile_rows * map_cols
    factor = 1.0 / math.sqrt(pixels * lax.axis_size("rows"))
    spatial = lax.all_to_all(output_grad, "rows", split_axis=0, concat_axis=2, tiled=True)
    masked_out = jnp.where(output_pre > 0, spatial, jnp.zeros_like(spatial))
    second_act = jnp.maximum(second_pre, jnp.zeros_like(second_pre))
    first_act = jnp.maximum(first_pre, jnp.zeros_like(first_pre))
    out_flat = masked_out.reshape(pixels, channels)
    last_part = contract_rows(second_act.reshape(pixels, inner_width), out_flat)
    last_total = lax.psum(last_part, "rows")
    inner = lax.dot_general(
        out_flat, last_weight, (((1,), (1,)), ((), ())), preferred_element_type=jnp.float32
    )
    second_grad = jnp.where(second_pre.reshape(pixels, inner_width) > 0, inner, 0.0).astype(
        jnp.bfloat16
    )
    second_flat = second_grad
    second_grad = second_flat.reshape(tile_rows, map_cols, inner_width)
    act_ext = with_halo(first_act, (("rows", 0),), 1)
    act_padded = jnp.pad(act_ext, ((0, 0), (1, 1), (0, 0)))
    taps = []
    for row_tap in range(3):
        line = []
        for col_tap in range(3):
            window = act_padded[
                row_tap : row_tap + tile_rows, col_tap : col_tap + map_cols
            ].reshape(pixels, inner_width)
            line.append(contract_rows(window, second_flat))
        taps.append(jnp.stack(line))
    middle_part = jnp.stack(taps)
    grad_ext = with_halo(second_grad, (("rows", 0),), 1)
    grad_padded = jnp.pad(grad_ext, ((0, 0), (1, 1), (0, 0)))
    total = jnp.zeros((pixels, inner_width), jnp.float32)
    for row_tap in range(3):
        for col_tap in range(3):
            moved = grad_padded[
                2 - row_tap : 2 - row_tap + tile_rows, 2 - col_tap : 2 - col_tap + map_cols
            ].reshape(pixels, inner_width)
            total = total + lax.dot_general(
                moved,
                middle_weight[row_tap, col_tap],
                (((1,), (1,)), ((), ())),
                preferred_element_type=jnp.float32,
            )
    first_grad = jnp.where(first_pre.reshape(pixels, inner_width) > 0, total, 0.0).astype(
        jnp.bfloat16
    )
    input_flat = block_input.reshape(pixels, channels)
    first_wgrad = (
        lax.psum_scatter(
            contract_rows(input_flat, first_grad), "rows", scatter_dimension=0, tiled=True
        )
        * factor
    )
    back = lax.dot_general(
        first_grad, first_weight, (((1,), (1,)), ((), ())), preferred_element_type=jnp.float32
    )
    input_grad = (
        (back + out_flat.astype(jnp.float32))
        .astype(jnp.bfloat16)
        .reshape(tile_rows, map_cols, channels)
    )
    middle_total = lax.psum(middle_part, "rows")
    return (input_grad, first_wgrad, middle_total * factor, last_total * factor)


def solution(mesh):
    placed = (
        P(("groups", "rows"), None, None),
        P(("groups", "rows"), None, None),
        P(("groups", "rows"), None, None),
        P(("groups", "rows"), None, None),
        P("groups", None, "rows"),
        P(),
        P(),
        P(),
    )
    return jax.shard_map(
        shards,
        mesh=mesh,
        in_specs=placed,
        out_specs=(
            P(("groups", "rows"), None, None),
            P(("groups", "rows"), None),
            P("groups", None, None, None),
            P("groups", None),
        ),
        check_vma=False,
    )
```

profile of v0, /device:TPU:0, one launch (start us, length us, event | category | flops | bytes accessed | tf_op | source)
XLA Modules:
  0.0 376.6 jit_solution(985985323894171516)
XLA Ops:
  7.2 9.7 %copy.21 = bf16[256,352,32]{1,2,0:T(8,128)(2,1)} copy(bf16[256,352,32]{0,2,1:T(8,128)(2,1)} %param.12) | data formatting | bytes 11534336 | tf_op args[4]
  16.8 7.6 %all-to-all-start = ((bf16[256,352,32]{1,2,0:T(8,128)(2,1)}), bf16[256,352,32]{1,2,0:T(8,128)(2,1)}, u32[]{:S(2)}, u32[]{:S(2)}) async-start(bf16[256,352,32]{1,2,0:T(8,128)(2,1)} %copy.21), calls=%async_computation | async-start | bytes 12582912 | tf_op jit(solution)/shard_map/all_to_all | solution.py:41
  24.6 2.4 collective-permute-start.2
  27.0 1.3 collective-permute-start.3
  28.3 1.3 broadcast_compare_fusion.1
  29.6 1.3 broadcast_compare_fusion
  30.9 8.3 %copy.20 = bf16[16,352,512]{1,2,0:T(8,128)(2,1)} copy(bf16[16,352,512]{2,1,0:T(8,128)(2,1)} %param.11) | data formatting | bytes 11534336 | tf_op args[3]
  39.2 1.7 pad_maximum_fusion.1
  41.4 3.9 %fusion.33 = (bf16[16,352,128]{2,1,0:T(8,128)(2,1)}, bf16[16,352,128]{2,1,0:T(8,128)(2,1)}, bf16[16,352,128]{2,1,0:T(8,128)(2,1)}, bf16[16,352,128]{2,1,0:T(8,12...) fusion(bf16[18,354,128]{2,1,0:T(8,128)(2,1)S(1)} %select_maximum_fusion), kind=kLoop, calls=%fused_computation.73 | loop fusion | bytes 17301504 | tf_op jit(solution)/shard_map/slice | solution.py:62
  45.3 93.3 %all-to-all-done = bf16[256,352,32]{1,2,0:T(8,128)(2,1)} async-done(((bf16[256,352,32]{1,2,0:T(8,128)(2,1)}), bf16[256,352,32]{1,2,0:T(8,128)(2,1)}, u32[]{:S(2)}, u32[]{:S(2)}) %all-to-all-start) | async-done | bytes 5767200 | tf_op jit(solution)/shard_map/all_to_all | solution.py:41
  138.6 6.4 %copy.22 = bf16[16,352,16,32]{1,3,2,0:T(8,128)(2,1)} copy(bf16[16,352,16,32]{1,3,0,2:T(8,128)(2,1)} %bitcast.3) | data formatting | bytes 11534336 | tf_op jit(solution)/shard_map/all_to_all | solution.py:41
  145.0 8.0 %compare_select_fusion = bf16[16,352,512]{1,2,0:T(8,128)(2,1)} fusion(bf16[16,352,512]{1,2,0:T(8,128)(2,1)} %copy.20, bf16[16,352,16,32]{1,3,2,0:T(8,128)(2,1)} %copy.22), kind=kLoop, calls=%fused_computation | loop fusion | flops 5767168 | bytes 17301504 | tf_op jit(solution)/shard_map/jit(_where)/select_n | solution.py:42
  153.1 8.5 %copy.23 = bf16[16,352,512]{2,1,0:T(8,128)(2,1)} copy(bf16[16,352,512]{1,2,0:T(8,128)(2,1)} %compare_select_fusion) | data formatting | bytes 11534336 | tf_op jit(solution)/shard_map/jit(_where)/select_n | solution.py:42
  161.6 5.8 %fusion.8 = f32[128,512]{1,0:T(8,128)} fusion(bf16[16,352,512]{1,2,0:T(8,128)(2,1)} %compare_select_fusion, bf16[16,352,128]{2,1,0:T(8,128)(2,1)S(1)} %copy-done.12), kind=kOutput, calls=%fused_computation.28 | convolution fusion | flops 738918400 | bytes 7471104 | tf_op jit(solution)/shard_map/dot_general | solution.py:22
  167.5 1.7 fusion.3
  179.9 2.7 collective-permute-start
  182.6 1.3 collective-permute-start.1
  185.0 8.5 %collective-permute-done.1 = bf16[1,352,128]{2,1,0:T(8,128)(2,1)S(1)} collective-permute-done((bf16[1,352,128]{2,1,0:T(8,128)(2,1)S(1)}, bf16[1,352,128]{2,1,0:T(8,128)(2,1)S(1)}, u32[]{:S(2)}, u32[]{:S(2)}) %collective-permute-start.1) | collective-permute-done | bytes 90144 | tf_op jit(solution)/shard_map/ppermute | solution.py:16
  194.1 2.4 fusion.34
  205.5 6.8 %add_convert_fusion = bf16[5632,512]{1,0:T(8,128)(2,1)} fusion(bf16[5632,512]{1,0:T(8,128)(2,1)} %bitcast.124, bf16[5632,128]{1,0:T(8,128)(2,1)S(1)} %fusion.2, bf16[512,128]{1,0:T(8,128)(2,1)S(1)} %copy-done), kind=kOutput, calls=%fused_computation.1 | convolution fusion | flops 746848256 | bytes 13107200 | tf_op jit(solution)/shard_map/dot_general | solution.py:92
  212.3 97.3 %all-reduce.5.cloned.1.call-done = (f32[3,3,128,128]{3,2,1,0:T(8,128)}, f32[128,512]{1,0:T(8,128)}) async-done(((f32[3,3,128,128]{3,2,1,0:T(8,128)}, f32[128,512]{1,0:T(8,128)}), (f32[3,3,128,128]{3,2,1,0:T(8,128)}, f32[128,512]{1,0:T(8,128)})) %all-reduce.5.cloned.1.call-update) | async-done | bytes 851984 | tf_op jit(solution)/shard_map/psum | solution.py:100
  309.6 1.7 broadcast_multiply_fusion.1
  311.3 1.9 broadcast_multiply_fusion
  313.2 55.1 %reduce-scatter.4.cloned.1.call-done = f32[32,128]{1,0:T(8,128)} async-done(((f32[512,128]{1,0:T(8,128)}), f32[32,128]{1,0:T(8,128)}) %reduce-scatter.4.cloned.1.call-update) | async-done | bytes 16400
  (78 shorter events, 23.3 us)
Async XLA Ops:
  7.2 198.3 %copy-start = (bf16[512,128]{1,0:T(8,128)(2,1)S(1)}, bf16[512,128]{1,0:T(8,128)(2,1)}, u32[]{:S(2)}) copy-start(bf16[512,128]{1,0:T(8,128)(2,1)} %param.13) | copy-start | bytes 393220
  16.8 7.6 %copy-start.2 = (bf16[16,352,128]{2,1,0:T(8,128)(2,1)S(1)}, bf16[16,352,128]{2,1,0:T(8,128)(2,1)}, u32[]{:S(2)}) copy-start(bf16[16,352,128]{2,1,0:T(8,128)(2,1)} %param.9) | copy-start | bytes 4325380
  16.8 121.8 %all-to-all-start = ((bf16[256,352,32]{1,2,0:T(8,128)(2,1)}), bf16[256,352,32]{1,2,0:T(8,128)(2,1)}, u32[]{:S(2)}, u32[]{:S(2)}) async-start(bf16[256,352,32]{1,2,0:T(8,128)(2,1)} %copy.21), calls=%async_computation | async-start | bytes 12582912 | tf_op jit(solution)/shard_map/all_to_all | solution.py:41
  24.4 285.2 %all-reduce.5.cloned.1.call-start = ((), (), s32[]{:S(2)}) async-start(), calls=%async_computation.3 | async-start | bytes 1703936 | tf_op jit(solution)/shard_map/psum | solution.py:100
  24.6 5.0 %copy-start.11 = (bf16[16,352,128]{2,1,0:T(8,128)(2,1)S(1)}, bf16[16,352,128]{2,1,0:T(8,128)(2,1)}, u32[]{:S(2)}) copy-start(bf16[16,352,128]{2,1,0:T(8,128)(2,1)} %param.10) | copy-start | bytes 4325380
  24.6 14.6 %collective-permute-start.2 = (bf16[1,352,128]{2,1,0:T(8,128)(2,1)S(1)}, bf16[1,352,128]{2,1,0:T(8,128)(2,1)S(1)}, u32[]{:S(2)}, u32[]{:S(2)}) collective-permute-start(bf16[1,352,128]{2,1,0:T(8,128)(2,1)S(1)} %get-tuple-element.32), channel_id=1, source_target_pairs={{0,1},{1,2},{2,3},{3,4},{4,5},{5,6},{6,7},{7,8},{8,9},{9,10},{10,1... | collective-permute-start | bytes 270344 | tf_op jit(solution)/shard_map/ppermute | solution.py:15
  27.0 12.2 %collective-permute-start.3 = (bf16[1,352,128]{2,1,0:T(8,128)(2,1)S(1)}, bf16[1,352,128]{2,1,0:T(8,128)(2,1)S(1)}, u32[]{:S(2)}, u32[]{:S(2)}) collective-permute-start(bf16[1,352,128]{2,1,0:T(8,128)(2,1)S(1)} %get-tuple-element.33), channel_id=1, source_target_pairs={{1,0},{2,1},{3,2},{4,3},{5,4},{6,5},{7,6},{8,7},{9,8},{10,9},{11,1... | collective-permute-start | bytes 270344 | tf_op jit(solution)/shard_map/ppermute | solution.py:16
  153.1 8.5 %copy-start.12 = (bf16[16,352,128]{2,1,0:T(8,128)(2,1)S(1)}, bf16[16,352,128]{2,1,0:T(8,128)(2,1)}, u32[]{:S(2)}) copy-start(bf16[16,352,128]{2,1,0:T(8,128)(2,1)} %param.10) | copy-start | bytes 4325380
  161.6 5.8 %copy-start.1 = (bf16[16,352,512]{2,1,0:T(8,128)(2,1)S(1)}, bf16[16,352,512]{2,1,0:T(8,128)(2,1)}, u32[]{:S(2)}) copy-start(bf16[16,352,512]{2,1,0:T(8,128)(2,1)} %copy.23) | copy-start | bytes 17301508
  161.6 5.8 %copy-start.14 = (pred[16,352,128]{2,1,0:T(32,128)(4,1)S(1)}, pred[16,352,128]{2,1,0:T(32,128)(4,1)}, u32[]{:S(2)}) copy-start(pred[16,352,128]{2,1,0:T(32,128)(4,1)} %broadcast_compare_fusion) | copy-start | bytes 2162692
  161.6 5.8 %copy-start.16 = (bf16[128,512]{1,0:T(8,128)(2,1)S(1)}, bf16[128,512]{1,0:T(8,128)(2,1)}, u32[]{:S(2)}) copy-start(bf16[128,512]{1,0:T(8,128)(2,1)} %param.15) | copy-start | bytes 393220
  167.5 1.7 copy-start.10
  169.2 1.4 copy-start.9
  170.5 1.4 copy-start.8
  171.9 1.4 copy-start.7
  173.3 1.4 copy-start.4
  175.2 1.4 copy-start.6
  176.6 1.4 copy-start.5
  179.9 5.2 %collective-permute-start = (bf16[1,352,128]{2,1,0:T(8,128)(2,1)S(1)}, bf16[1,352,128]{2,1,0:T(8,128)(2,1)S(1)}, u32[]{:S(2)}, u32[]{:S(2)}) collective-permute-start(bf16[1,352,128]{2,1,0:T(8,128)(2,1)S(1)} %get-tuple-element.36), channel_id=1, source_target_pairs={{0,1},{1,2},{2,3},{3,4},{4,5},{5,6},{6,7},{7,8},{8,9},{9,10},{10,1... | collective-permute-start | bytes 270344 | tf_op jit(solution)/shard_map/ppermute | solution.py:15
  182.6 11.0 %collective-permute-start.1 = (bf16[1,352,128]{2,1,0:T(8,128)(2,1)S(1)}, bf16[1,352,128]{2,1,0:T(8,128)(2,1)S(1)}, u32[]{:S(2)}, u32[]{:S(2)}) collective-permute-start(bf16[1,352,128]{2,1,0:T(8,128)(2,1)S(1)} %get-tuple-element.37), channel_id=1, source_target_pairs={{1,0},{2,1},{3,2},{4,3},{5,4},{6,5},{7,6},{8,7},{9,8},{10,9},{11,1... | collective-permute-start | bytes 270344 | tf_op jit(solution)/shard_map/ppermute | solution.py:16
  184.8 183.4 %reduce-scatter.4.cloned.1.call-start = ((), (), s32[]{:S(2)}) async-start(), calls=%async_computation.2 | async-start | bytes 278528
  194.1 2.4 copy-start.15
  200.5 2.4 slice-start
  201.6 2.0 slice-start.1
  (2 other events, 2.5 us)
Sparse Core Ops, SparseCore 0:
  184.9 124.6 all-reduce.4
  313.1 55.1 reduce-scatter.3
where the time goes:
time: 378 us; the launch traced here: 377 us
  waiting for transfers between devices  254 us (67%)
  local copies, waits for them, and re-layouts  48.8 us (13%)
  matrix products  25.6 us (7%)
  other arithmetic  18 us (5%)
  starting transfers between devices  15.5 us (4%)
  between operations  14.4 us (4%)
    psum x1, waiting for transfers between devices, shards(): middle_total = lax.psum(middle_part, 'rows')  97.3 us
    all_to_all x1, waiting for transfers between devices, shards(): lax.all_to_all(output_grad, 'rows', split_axis=0, concat_axis=2, tiled=True)  93.3 us
    unnamed x3, waiting for transfers between devices  55.1 us
    unnamed x43, local copies, waits for them, and re-layouts  27.6 us
    dot_general x11, matrix products, contract_rows(): lax.dot_general(left, right, (((0,), (0,)), ((), ())), preferred_element_...  12 us
    ppermute x2, waiting for transfers between devices, with_halo(): after = lax.ppermute(leading, axis, down)  8.54 us
    select_n x1, local copies, waits for them, and re-layouts, shards(): masked_out = jnp.where(output_pre > 0, spatial, jnp.zeros_like(spatial))  8.53 us
    select_n x1, other arithmetic, shards(): masked_out = jnp.where(output_pre > 0, spatial, jnp.zeros_like(spatial))  8.04 us
  transfers between devices with their start and end apart: 7, of which 4 were waited for; matrix products, arithmetic and copies ran while one was open for 10% of the time, Pallas kernels for 0%

commit v1 on v0

--- a/solution.py
+++ b/solution.py
@@ -38,7 +38,12 @@
     inner_width = first_pre.shape[2]
     pixels = tile_rows * map_cols
     factor = 1.0 / math.sqrt(pixels * lax.axis_size("rows"))
-    spatial = lax.all_to_all(output_grad, "rows", split_axis=0, concat_axis=2, tiled=True)
+    spatial = jnp.concatenate(
+        lax.all_to_all(
+            jnp.stack(jnp.split(output_grad, lax.axis_size("rows"), axis=0)), "rows", 0, 0
+        ),
+        axis=2,
+    )
     masked_out = jnp.where(output_pre > 0, spatial, jnp.zeros_like(spatial))
     second_act = jnp.maximum(second_pre, jnp.zeros_like(second_pre))
     first_act = jnp.maximum(first_pre, jnp.zeros_like(first_pre))

time: 378 us -> 507 us (1.34); the launches traced: 377 us -> 497 us
  local copies, waits for them, and re-layouts: 48.8 us -> 171 us
    unnamed x43 -> x101, local copies, waits for them, and re-layouts: 27.6 us -> 121 us
    split x0 -> x1, local copies, waits for them, and re-layouts: none -> 30.5 us  [shards(): jnp.split(output_grad, lax.axis_size('rows'), axis=0)]
    all_to_all x1 -> x0, local copies, waits for them, and re-layouts: 6.43 us -> none  [shards(): lax.all_to_all(output_grad, 'rows', split_axis=0, concat_axis=2, tiled=True)]
  transfers between devices with their start and end apart: 7 -> 7, of which waited for: 4 -> 4; matrix products, arithmetic and copies ran while one was open for 10% -> 8% of each run, Pallas kernels for 0% -> 0%
where the time goes in v1:
time: 507 us; the launch traced here: 497 us
  waiting for transfers between devices  254 us (50%)
  local copies, waits for them, and re-layouts  171 us (34%)
  matrix products  25.6 us (5%)
  other arithmetic  16.3 us (3%)
  starting transfers between devices  15.4 us (3%)
  between operations  14.7 us (3%)
    unnamed x101, local copies, waits for them, and re-layouts  121 us
    psum x1, waiting for transfers between devices, shards(): middle_total = lax.psum(middle_part, 'rows')  97.2 us
    all_to_all x1, waiting for transfers between devices, shards(): lax.all_to_all(jnp.stack(jnp.split(output_grad, lax.axis_size('rows'), ax...  93 us
    unnamed x3, waiting for transfers between devices  55.1 us
    split x1, local copies, waits for them, and re-layouts, shards(): jnp.split(output_grad, lax.axis_size('rows'), axis=0)  30.5 us
    dot_general x11, matrix products, contract_rows(): lax.dot_general(left, right, (((0,), (0,)), ((), ())), preferred_element_...  12 us
  transfers between devices with their start and end apart: 7, of which 4 were waited for; matrix products, arithmetic and copies ran while one was open for 8% of the time, Pallas kernels for 0%

profile of v1, /device:TPU:0, one launch (start us, length us, event | category | flops | bytes accessed | tf_op | source)
XLA Modules:
  0.0 497.2 jit_solution(3860013397703689160)
XLA Ops:
  7.2 30.5 %fusion.33 = (bf16[16,352,32]{0,2,1:T(8,128)(2,1)S(1)}, bf16[16,352,32]{0,2,1:T(8,128)(2,1)}, bf16[16,352,32]{0,2,1:T(8,128)(2,1)}, bf16[16,352,32]{0,2,1:T(8,12...) fusion(bf16[256,352,32]{0,2,1:T(8,128)(2,1)} %param.12), kind=kLoop, calls=%fused_computation.89 | loop fusion | bytes 11534336 | tf_op jit(solution)/shard_map/split | solution.py:43
  43.7 5.8 %copy.43 = bf16[16,352,32]{1,2,0:T(8,128)(2,1)} copy(bf16[16,352,32]{0,2,1:T(8,128)(2,1)} %get-tuple-element.32) | data formatting | bytes 720896
  49.4 5.8 %copy.44 = bf16[16,352,32]{1,2,0:T(8,128)(2,1)} copy(bf16[16,352,32]{0,2,1:T(8,128)(2,1)} %get-tuple-element.31) | data formatting | bytes 720896
  55.2 5.8 %copy.45 = bf16[16,352,32]{1,2,0:T(8,128)(2,1)} copy(bf16[16,352,32]{0,2,1:T(8,128)(2,1)} %get-tuple-element.30) | data formatting | bytes 720896
  61.0 5.8 %copy.46 = bf16[16,352,32]{1,2,0:T(8,128)(2,1)} copy(bf16[16,352,32]{0,2,1:T(8,128)(2,1)} %get-tuple-element.29) | data formatting | bytes 720896
  66.8 5.8 %copy.47 = bf16[16,352,32]{1,2,0:T(8,128)(2,1)} copy(bf16[16,352,32]{0,2,1:T(8,128)(2,1)} %get-tuple-element.28) | data formatting | bytes 720896
  72.6 6.0 %copy.48 = bf16[16,352,32]{1,2,0:T(8,128)(2,1)} copy(bf16[16,352,32]{0,2,1:T(8,128)(2,1)} %get-tuple-element.27) | data formatting | bytes 720896
  78.5 5.8 %copy.49 = bf16[16,352,32]{1,2,0:T(8,128)(2,1)} copy(bf16[16,352,32]{0,2,1:T(8,128)(2,1)} %get-tuple-element.26) | data formatting | bytes 720896
  84.3 5.8 %copy.50 = bf16[16,352,32]{1,2,0:T(8,128)(2,1)} copy(bf16[16,352,32]{0,2,1:T(8,128)(2,1)} %get-tuple-element.25) | data formatting | bytes 720896
  90.1 5.8 %copy.51 = bf16[16,352,32]{1,2,0:T(8,128)(2,1)} copy(bf16[16,352,32]{0,2,1:T(8,128)(2,1)} %get-tuple-element.24) | data formatting | bytes 720896
  95.9 5.8 %copy.52 = bf16[16,352,32]{1,2,0:T(8,128)(2,1)} copy(bf16[16,352,32]{0,2,1:T(8,128)(2,1)} %get-tuple-element.23) | data formatting | bytes 720896
  101.6 5.8 %copy.53 = bf16[16,352,32]{1,2,0:T(8,128)(2,1)} copy(bf16[16,352,32]{0,2,1:T(8,128)(2,1)} %get-tuple-element.22) | data formatting | bytes 720896
  107.4 5.8 %copy.54 = bf16[16,352,32]{1,2,0:T(8,128)(2,1)} copy(bf16[16,352,32]{0,2,1:T(8,128)(2,1)} %get-tuple-element.21) | data formatting | bytes 720896
  113.2 5.8 %copy.55 = bf16[16,352,32]{1,2,0:T(8,128)(2,1)} copy(bf16[16,352,32]{0,2,1:T(8,128)(2,1)} %get-tuple-element.20) | data formatting | bytes 720896
  143.2 7.6 %all-to-all-start = ((bf16[16,16,352,32]{2,3,1,0:T(8,128)(2,1)}), bf16[16,16,352,32]{2,3,1,0:T(8,128)(2,1)}, u32[]{:S(2)}, u32[]{:S(2)}) async-start(bf16[16,16,352,32]{2,3,1,0:T(8,128)(2,1)} %bitcast_dynamic-update-slice_fusion), calls=%async_computation | async-start | bytes 12582912 | tf_op jit(solution)/shard_map/all_to_all | solution.py:42
  157.4 8.4 %copy.18 = bf16[16,352,512]{1,2,0:T(8,128)(2,1)} copy(bf16[16,352,512]{2,1,0:T(8,128)(2,1)} %param.11) | data formatting | bytes 11534336 | tf_op args[3]
  172.0 93.0 %all-to-all-done = bf16[16,16,352,32]{2,3,1,0:T(8,128)(2,1)} async-done(((bf16[16,16,352,32]{2,3,1,0:T(8,128)(2,1)}), bf16[16,16,352,32]{2,3,1,0:T(8,128)(2,1)}, u32[]{:S(2)}, u32[]{:S(2)}) %all-to-all-start) | async-done | bytes 5767200 | tf_op jit(solution)/shard_map/all_to_all | solution.py:42
  268.7 6.2 %compare_select_fusion = bf16[16,352,512]{1,2,0:T(8,128)(2,1)} fusion(bf16[16,352,512]{1,2,0:T(8,128)(2,1)} %copy.18, bf16[16,352,16,32]{1,3,2,0:T(8,128)(2,1)S(1)} %copy.35), kind=kLoop, calls=%fused_computation | loop fusion | flops 5767168 | bytes 17301504 | tf_op jit(solution)/shard_map/jit(_where)/select_n | solution.py:47
  274.9 8.9 %copy.36 = bf16[16,352,512]{2,1,0:T(8,128)(2,1)} copy(bf16[16,352,512]{1,2,0:T(8,128)(2,1)} %compare_select_fusion) | data formatting | bytes 11534336 | tf_op jit(solution)/shard_map/jit(_where)/select_n | solution.py:47
  283.9 5.8 %fusion.8 = f32[128,512]{1,0:T(8,128)} fusion(bf16[16,352,512]{1,2,0:T(8,128)(2,1)} %compare_select_fusion, bf16[16,352,128]{2,1,0:T(8,128)(2,1)S(1)} %copy-done.14), kind=kOutput, calls=%fused_computation.28 | convolution fusion | flops 738918400 | bytes 7471104 | tf_op jit(solution)/shard_map/dot_general | solution.py:22
  305.3 8.7 %collective-permute-done.1 = bf16[1,352,128]{2,1,0:T(8,128)(2,1)S(1)} collective-permute-done((bf16[1,352,128]{2,1,0:T(8,128)(2,1)S(1)}, bf16[1,352,128]{2,1,0:T(8,128)(2,1)S(1)}, u32[]{:S(2)}, u32[]{:S(2)}) %collective-permute-start.1) | collective-permute-done | bytes 90144 | tf_op jit(solution)/shard_map/ppermute | solution.py:16
  326.0 6.8 %add_convert_fusion = bf16[5632,512]{1,0:T(8,128)(2,1)} fusion(bf16[5632,512]{1,0:T(8,128)(2,1)} %bitcast.154, bf16[5632,128]{1,0:T(8,128)(2,1)S(1)} %fusion.2, bf16[512,128]{1,0:T(8,128)(2,1)S(1)} %copy-done), kind=kOutput, calls=%fused_computation.1 | convolution fusion | flops 746848256 | bytes 13107200 | tf_op jit(solution)/shard_map/dot_general | solution.py:97
  332.9 97.2 %all-reduce.5.cloned.1.call-done = (f32[3,3,128,128]{3,2,1,0:T(8,128)}, f32[128,512]{1,0:T(8,128)}) async-done(((f32[3,3,128,128]{3,2,1,0:T(8,128)}, f32[128,512]{1,0:T(8,128)}), (f32[3,3,128,128]{3,2,1,0:T(8,128)}, f32[128,512]{1,0:T(8,128)})) %all-reduce.5.cloned.1.call-update) | async-done | bytes 851984 | tf_op jit(solution)/shard_map/psum | solution.py:105
  433.6 55.1 %reduce-scatter.4.cloned.1.call-done = f32[32,128]{1,0:T(8,128)} async-done(((f32[512,128]{1,0:T(8,128)}), f32[32,128]{1,0:T(8,128)}) %reduce-scatter.4.cloned.1.call-update) | async-done | bytes 16400
  (138 shorter events, 78.9 us)
Async XLA Ops:
  7.2 318.8 %copy-start = (bf16[512,128]{1,0:T(8,128)(2,1)S(1)}, bf16[512,128]{1,0:T(8,128)(2,1)}, u32[]{:S(2)}) copy-start(bf16[512,128]{1,0:T(8,128)(2,1)} %param.13) | copy-start | bytes 393220
  129.0 3.7 copy-start.28
  129.0 4.6 copy-start.27
  129.0 5.4 %copy-start.26 = (bf16[16,352,32]{1,2,0:T(8,128)(2,1)S(1)}, bf16[16,352,32]{1,2,0:T(8,128)(2,1)}, u32[]{:S(2)}) copy-start(bf16[16,352,32]{1,2,0:T(8,128)(2,1)} %copy.47) | copy-start | bytes 1081348
  130.9 4.3 copy-start.25
  132.7 3.2 copy-start.24
  134.4 3.2 copy-start.22
  136.0 3.2 copy-start.20
  136.8 3.2 copy-start.19
  137.6 3.2 copy-start.18
  143.2 7.6 %copy-start.4 = (bf16[16,352,128]{2,1,0:T(8,128)(2,1)S(1)}, bf16[16,352,128]{2,1,0:T(8,128)(2,1)}, u32[]{:S(2)}) copy-start(bf16[16,352,128]{2,1,0:T(8,128)(2,1)} %param.9) | copy-start | bytes 4325380
  143.2 121.8 %all-to-all-start = ((bf16[16,16,352,32]{2,3,1,0:T(8,128)(2,1)}), bf16[16,16,352,32]{2,3,1,0:T(8,128)(2,1)}, u32[]{:S(2)}, u32[]{:S(2)}) async-start(bf16[16,16,352,32]{2,3,1,0:T(8,128)(2,1)} %bitcast_dynamic-update-slice_fusion), calls=%async_computation | async-start | bytes 12582912 | tf_op jit(solution)/shard_map/all_to_all | solution.py:42
  150.7 279.3 %all-reduce.5.cloned.1.call-start = ((), (), s32[]{:S(2)}) async-start(), calls=%async_computation.3 | async-start | bytes 1703936 | tf_op jit(solution)/shard_map/psum | solution.py:105
  150.9 16.7 %copy-start.2 = (bf16[16,352,128]{2,1,0:T(8,128)(2,1)}, bf16[16,352,128]{2,1,0:T(8,128)(2,1)S(1)}, u32[]{:S(2)}) copy-start(bf16[16,352,128]{2,1,0:T(8,128)(2,1)S(1)} %broadcast_maximum_fusion) | copy-start | bytes 4325380
  150.9 5.2 %copy-start.13 = (bf16[16,352,128]{2,1,0:T(8,128)(2,1)S(1)}, bf16[16,352,128]{2,1,0:T(8,128)(2,1)}, u32[]{:S(2)}) copy-start(bf16[16,352,128]{2,1,0:T(8,128)(2,1)} %param.10) | copy-start | bytes 4325380
  150.9 14.9 %collective-permute-start.2 = (bf16[1,352,128]{2,1,0:T(8,128)(2,1)S(1)}, bf16[1,352,128]{2,1,0:T(8,128)(2,1)S(1)}, u32[]{:S(2)}, u32[]{:S(2)}) collective-permute-start(bf16[1,352,128]{2,1,0:T(8,128)(2,1)S(1)} %get-tuple-element.48), channel_id=1, source_target_pairs={{0,1},{1,2},{2,3},{3,4},{4,5},{5,6},{6,7},{7,8},{8,9},{9,10},{10,1... | collective-permute-start | bytes 270344 | tf_op jit(solution)/shard_map/ppermute | solution.py:15
  153.5 12.3 %collective-permute-start.3 = (bf16[1,352,128]{2,1,0:T(8,128)(2,1)S(1)}, bf16[1,352,128]{2,1,0:T(8,128)(2,1)S(1)}, u32[]{:S(2)}, u32[]{:S(2)}) collective-permute-start(bf16[1,352,128]{2,1,0:T(8,128)(2,1)S(1)} %get-tuple-element.49), channel_id=1, source_target_pairs={{1,0},{2,1},{3,2},{4,3},{5,4},{6,5},{7,6},{8,7},{9,8},{10,9},{11,1... | collective-permute-start | bytes 270344 | tf_op jit(solution)/shard_map/ppermute | solution.py:16
  274.9 8.9 %copy-start.14 = (bf16[16,352,128]{2,1,0:T(8,128)(2,1)S(1)}, bf16[16,352,128]{2,1,0:T(8,128)(2,1)}, u32[]{:S(2)}) copy-start(bf16[16,352,128]{2,1,0:T(8,128)(2,1)} %param.10) | copy-start | bytes 4325380
  283.9 5.9 %copy-start.1 = (bf16[16,352,512]{2,1,0:T(8,128)(2,1)S(1)}, bf16[16,352,512]{2,1,0:T(8,128)(2,1)}, u32[]{:S(2)}) copy-start(bf16[16,352,512]{2,1,0:T(8,128)(2,1)} %copy.36) | copy-start | bytes 17301508
  283.9 5.9 %copy-start.16 = (pred[16,352,128]{2,1,0:T(32,128)(4,1)S(1)}, pred[16,352,128]{2,1,0:T(32,128)(4,1)}, u32[]{:S(2)}) copy-start(pred[16,352,128]{2,1,0:T(32,128)(4,1)} %broadcast_compare_fusion) | copy-start | bytes 2162692
  283.9 5.8 %copy-start.30 = (bf16[128,512]{1,0:T(8,128)(2,1)S(1)}, bf16[128,512]{1,0:T(8,128)(2,1)}, u32[]{:S(2)}) copy-start(bf16[128,512]{1,0:T(8,128)(2,1)} %param.15) | copy-start | bytes 393220
  300.3 5.0 %collective-permute-start = (bf16[1,352,128]{2,1,0:T(8,128)(2,1)S(1)}, bf16[1,352,128]{2,1,0:T(8,128)(2,1)S(1)}, u32[]{:S(2)}, u32[]{:S(2)}) collective-permute-start(bf16[1,352,128]{2,1,0:T(8,128)(2,1)S(1)} %get-tuple-element.52), channel_id=1, source_target_pairs={{0,1},{1,2},{2,3},{3,4},{4,5},{5,6},{6,7},{7,8},{8,9},{9,10},{10,1... | collective-permute-start | bytes 270344 | tf_op jit(solution)/shard_map/ppermute | solution.py:15
  303.0 11.0 %collective-permute-start.1 = (bf16[1,352,128]{2,1,0:T(8,128)(2,1)S(1)}, bf16[1,352,128]{2,1,0:T(8,128)(2,1)S(1)}, u32[]{:S(2)}, u32[]{:S(2)}) collective-permute-start(bf16[1,352,128]{2,1,0:T(8,128)(2,1)S(1)} %get-tuple-element.53), channel_id=1, source_target_pairs={{1,0},{2,1},{3,2},{4,3},{5,4},{6,5},{7,6},{8,7},{9,8},{10,9},{11,1... | collective-permute-start | bytes 270344 | tf_op jit(solution)/shard_map/ppermute | solution.py:16
  305.2 183.5 %reduce-scatter.4.cloned.1.call-start = ((), (), s32[]{:S(2)}) async-start(), calls=%async_computation.2 | async-start | bytes 278528
  (16 other events, 30.9 us)
Sparse Core Ops, SparseCore 0:
  305.3 124.6 all-reduce.4
  433.5 55.1 reduce-scatter.3
